TPU v7x, 128 devices: a whole 4x4x4 slice. The times are simulated.
128 devices in a mesh: outer: 4 (over x), ctr: 32 (over y, z, core).
Axes of the slice: x: 4, y: 4, z: 4, core: 2. Of those that a mesh axis runs over, the one named last changes fastest.
Arguments:
- amplitudes: float32 [1024, 131072], P(('outer', 'ctr')), may hold values from -24 to 24
- integrals: float32 [4096, 131072], P('outer', 'ctr'), may hold values from -0.015625 to 0.015625
- block_mask: int32 [32, 1024], P('outer', 'ctr'), may hold values 0 or 1
Outputs:
- ladder: float32 [1024, 4096], P('ctr', 'outer')
All inputs are finite; a program needn't handle non-finite values. No bound on the sum of `block_mask` on one device may be relied on, other than what follows from the above.
Results may differ from a plain program's by a relative error of at most 0.000071.
Values sent between devices are 32-bit elements; how exact they have to be, the bound alone decides.
A program may use at most 128 MiB of HBM per device.

v0:
```python
import jax
import jax.numpy as jnp
from jax import lax
from jax.sharding import PartitionSpec as P


def local(amplitudes, integrals, block_mask):
    ab_rows = integrals.shape[0]
    cd_cols = integrals.shape[1]
    ab_blocks = block_mask.shape[0]
    cd_blocks = block_mask.shape[1]
    tile_rows = ab_rows // ab_blocks
    tile_cols = cd_cols // cd_blocks
    mask_f = block_mask.astype(jnp.float32)
    shaped = integrals.reshape(ab_blocks, tile_rows, cd_blocks, tile_cols)
    sparse_v = (shaped * mask_f[:, None, :, None]).reshape(ab_rows, cd_cols)
    local_rows = lax.all_to_all(amplitudes, "ctr", split_axis=1, concat_axis=0, tiled=True)
    partial_terms = lax.dot_general(
        lax.all_gather(local_rows, "outer", axis=0, tiled=True),
        sparse_v,
        (((1,), (1,)), ((), ())),
        precision=lax.Precision.HIGHEST,
        preferred_element_type=jnp.float32,
    )
    summed = lax.psum(partial_terms, "ctr")
    own_rows = summed.shape[0] // lax.axis_size("ctr")
    offset = lax.axis_index("ctr") * own_rows
    result = lax.dynamic_slice_in_dim(summed, offset, own_rows, 0)
    return result


def solution(mesh):
    return jax.shard_map(
        local,
        mesh=mesh,
        in_specs=(P(("outer", "ctr"), None), P("outer", "ctr"), P("outer", "ctr")),
        out_specs=P("ctr", "outer"),
        check_vma=False,
    )
```

profile of v0, /device:TPU:1, one launch (start us, length us, event | category | flops | bytes accessed | tf_op | source)
XLA Modules:
  0.0 415.4 jit_solution(17326440921595013472)
XLA Ops:
  6.5 0.0 all-gather.2.cloned.1.call-start
  6.5 60.3 %all_to_all.19 = f32[8,32,4096]{2,0,1:T(8,128)} all-to-all(f32[8,32,4096]{2,0,1:T(8,128)} %bitcast.20), channel_id=1, replica_groups=mesh['outer'=4,'ctr'=32] {'ctr'}, dimensions={1} | all-to-all | bytes 8388608 | tf_op jit(solution)/shard_map/all_to_all | solution.py:17
  66.8 0.0 all-gather.2.cloned.1.call-update
  66.9 0.0 all-reduce.2.cloned.1.call-start
  66.9 0.7 convert_element_type.3
  67.6 150.8 %all-gather.2.cloned.1.call-done = f32[1024,4096]{1,0:T(8,128)} async-done(((f32[256,4096]{1,0:T(8,128)}), f32[1024,4096]{1,0:T(8,128)}) %all-gather.2.cloned.1.call-update) | async-done | bytes 16777232 | tf_op jit(solution)/shard_map/all_gather | solution.py:19
  218.4 2.2 mul.14
  220.6 72.8 %fusion.2 = f32[1024,1024]{0,1:T(8,128)} fusion(f32[1024,4096]{1,0:T(8,128)} %all-gather.2.cloned.1.call-done, f32[1024,4096]{1,0:T(8,128)} %param.4, f32[128,8,32,128]{3,2,1,0:T(8,128)S(1)} %bitcast.18), kind=kOutput, calls=%fused_computation.3 | convolution fusion | flops 51543801856 | bytes 54525952 | tf_op jit(solution)/shard_map/dot_general | solution.py:18
  293.4 0.0 all-reduce.2.cloned.1.call-update
  293.4 113.1 %all-reduce.2.cloned.1.call-done = f32[1024,1024]{0,1:T(8,128)} async-done(((f32[1024,1024]{0,1:T(8,128)}), f32[1024,1024]{0,1:T(8,128)}) %all-reduce.2.cloned.1.call-update) | async-done | bytes 4194320 | tf_op jit(solution)/shard_map/psum | solution.py:25
  406.5 1.2 constant_dynamic-slice_fusion
  407.7 0.8 copy.4
Async XLA Ops:
  6.5 211.9 %all-gather.2.cloned.1.call-start = ((), (), s32[]{:S(2)}) async-start(), calls=%async_computation.1 | async-start | bytes 20971520 | tf_op jit(solution)/shard_map/all_gather | solution.py:19
  66.9 339.6 %all-reduce.2.cloned.1.call-start = ((), (), s32[]{:S(2)}) async-start(), calls=%async_computation.2 | async-start | bytes 8388608 | tf_op jit(solution)/shard_map/psum | solution.py:25
Sparse Core Ops, SparseCore 0:
  67.0 151.3 all-gather.1
  293.6 112.9 all-reduce.1
where the time goes:
time: 416 us; the launch traced here: 415 us
  waiting for transfers between devices  264 us (63%)
  matrix products  72.8 us (18%)
  blocking collectives  60.3 us (14%)
  between operations  13.4 us (3%)
  local copies, waits for them, and re-layouts  4.28 us (1%)
    all_gather x1, waiting for transfers between devices, local(): lax.all_gather(local_rows, 'outer', axis=0, tiled=True)  151 us
    psum x1, waiting for transfers between devices, local(): summed = lax.psum(partial_terms, 'ctr')  113 us
    dot_general x1, matrix products, local(): lax.dot_general(lax.all_gather(local_rows, 'outer', axis=0, tiled=True),...  72.8 us
    all_to_all x1, blocking collectives, local(): lax.all_to_all(amplitudes, 'ctr', split_axis=1, concat_axis=0, tiled=True)  60.3 us
  transfers between devices with their start and end apart: 2, of which 2 were waited for; matrix products, arithmetic and copies ran while one was open for 0% of the time, Pallas kernels for 0%

commit v1 on v0

--- a/solution.py
+++ b/solution.py
@@ -15,8 +15,12 @@
     shaped = integrals.reshape(ab_blocks, tile_rows, cd_blocks, tile_cols)
     sparse_v = (shaped * mask_f[:, None, :, None]).reshape(ab_rows, cd_cols)
     local_rows = lax.all_to_all(amplitudes, "ctr", split_axis=1, concat_axis=0, tiled=True)
+    leaves_do = lambda frame_in: jnp.concatenate(
+        lax.all_to_all(jnp.stack(lax.axis_size("outer") * [frame_in], axis=0), "outer", 0, 0),
+        axis=0,
+    )
     partial_terms = lax.dot_general(
-        lax.all_gather(local_rows, "outer", axis=0, tiled=True),
+        leaves_do(local_rows),
         sparse_v,
         (((1,), (1,)), ((), ())),
         precision=lax.Precision.HIGHEST,

time: 416 us -> 458 us (1.10)
  waiting for transfers between devices: 264 us -> 292 us
  local copies, waits for them, and re-layouts: 4.28 us -> 12.1 us
  starting transfers between devices: 0.04 us -> 7.15 us
    all_to_all x0 -> x1, waiting for transfers between devices: none -> 184 us  [local(): lax.all_to_all(jnp.stack(lax.axis_size('outer') * [frame_in], axis=0), 'o...]
    all_gather x1 -> x0, waiting for transfers between devices: 151 us -> none  [local(): lax.all_gather(local_rows, 'outer', axis=0, tiled=True)]
    another operation x0 -> x1, local copies, waits for them, and re-layouts: none -> 7.81 us  [local(): jnp.stack(lax.axis_size('outer') * [frame_in], axis=0)]
    all_to_all x0 -> x1, starting transfers between devices: none -> 7.11 us  [local(): lax.all_to_all(jnp.stack(lax.axis_size('outer') * [frame_in], axis=0), 'o...]
    psum x1, waiting for transfers between devices: 113 us -> 108 us  [local(): summed = lax.psum(partial_terms, 'ctr')]
where the time goes in v1:
time: 458 us
  waiting for transfers between devices  292 us (64%)
  matrix products  73 us (16%)
  blocking collectives  60.2 us (13%)
  between operations  13.4 us (3%)
  local copies, waits for them, and re-layouts  12.1 us (3%)
  starting transfers between devices  7.15 us (2%)
    all_to_all x1, waiting for transfers between devices, local(): lax.all_to_all(jnp.stack(lax.axis_size('outer') * [frame_in], axis=0), 'o...  184 us
    psum x1, waiting for transfers between devices, local(): summed = lax.psum(partial_terms, 'ctr')  108 us
    dot_general x1, matrix products, local(): lax.dot_general(leaves_do(local_rows), sparse_v, (((1,), (1,)), ((), ()))...  73 us
    all_to_all x1, blocking collectives, local(): lax.all_to_all(amplitudes, 'ctr', split_axis=1, concat_axis=0, tiled=True)  60.2 us
  transfers between devices with their start and end apart: 2, of which 2 were waited for; matrix products, arithmetic and copies ran while one was open for 0% of the time, Pallas kernels for 0%

profile of v1, /device:TPU:1, one launch (start us, length us, event | category | flops | bytes accessed | tf_op | source)
XLA Modules:
  0.0 457.6 jit_solution(3263891169555534720)
XLA Ops:
  6.5 60.2 %all_to_all.21 = f32[8,32,4096]{2,0,1:T(8,128)S(1)} all-to-all(f32[8,32,4096]{2,0,1:T(8,128)} %bitcast.21), channel_id=1, replica_groups=mesh['outer'=4,'ctr'=32] {'ctr'}, dimensions={1} | all-to-all | bytes 8388608 | tf_op jit(solution)/shard_map/all_to_all | solution.py:17
  66.7 7.8 %stack.10 = f32[4,256,4096]{2,1,0:T(8,128)} broadcast(f32[256,4096]{1,0:T(8,128)S(1)} %bitcast.19), dimensions={1,2} | broadcast | bytes 20971520 | tf_op jit(solution)/shard_map/stack | solution.py:19
  74.6 0.0 copy-start
  74.6 7.1 %all-to-all-start.1 = ((f32[4,256,4096]{2,1,0:T(8,128)}), f32[4,256,4096]{2,1,0:T(8,128)}, u32[]{:S(2)}, u32[]{:S(2)}) async-start(f32[4,256,4096]{2,1,0:T(8,128)} %stack.10), calls=%async_computation.1 | async-start | bytes 33554432 | tf_op jit(solution)/shard_map/all_to_all | solution.py:19
  81.7 0.0 all-reduce.2.cloned.1.call-start
  81.7 0.0 copy-done
  81.7 183.6 %all-to-all-done.1 = f32[4,256,4096]{2,1,0:T(8,128)} async-done(((f32[4,256,4096]{2,1,0:T(8,128)}), f32[4,256,4096]{2,1,0:T(8,128)}, u32[]{:S(2)}, u32[]{:S(2)}) %all-to-all-start.1) | async-done | bytes 16777248 | tf_op jit(solution)/shard_map/all_to_all | solution.py:19
  265.3 2.2 mul.14
  267.5 73.0 %fusion.2 = f32[1024,1024]{0,1:T(8,128)} fusion(f32[1024,4096]{1,0:T(8,128)} %bitcast.3, f32[1024,4096]{1,0:T(8,128)} %param.4, f32[128,8,32,128]{3,2,1,0:T(8,128)S(1)} %bitcast.20), kind=kOutput, calls=%fused_computation.3 | convolution fusion | flops 51543801856 | bytes 54525952 | tf_op jit(solution)/shard_map/dot_general | solution.py:22
  340.5 0.0 all-reduce.2.cloned.1.call-update
  340.6 108.1 %all-reduce.2.cloned.1.call-done = f32[1024,1024]{0,1:T(8,128)} async-done(((f32[1024,1024]{0,1:T(8,128)}), f32[1024,1024]{0,1:T(8,128)}) %all-reduce.2.cloned.1.call-update) | async-done | bytes 4194320 | tf_op jit(solution)/shard_map/psum | solution.py:29
  448.7 1.2 constant_dynamic-slice_fusion
  449.9 0.8 copy.4
  (1 shorter events, 0.0 us)
Async XLA Ops:
  74.6 7.2 %copy-start = (s32[8,32]{1,0:T(8,128)S(1)}, s32[8,32]{1,0:T(8,128)}, u32[]{:S(2)}) copy-start(s32[8,32]{1,0:T(8,128)} %param.5) | copy-start | bytes 3076
  74.6 190.8 %all-to-all-start.1 = ((f32[4,256,4096]{2,1,0:T(8,128)}), f32[4,256,4096]{2,1,0:T(8,128)}, u32[]{:S(2)}, u32[]{:S(2)}) async-start(f32[4,256,4096]{2,1,0:T(8,128)} %stack.10), calls=%async_computation.1 | async-start | bytes 33554432 | tf_op jit(solution)/shard_map/all_to_all | solution.py:19
  81.7 367.0 %all-reduce.2.cloned.1.call-start = ((), (), s32[]{:S(2)}) async-start(), calls=%async_computation.2 | async-start | bytes 8388608 | tf_op jit(solution)/shard_map/psum | solution.py:29
Sparse Core Ops, SparseCore 0:
  340.7 107.9 all-reduce.1

commit v2 on v0

--- a/solution.py
+++ b/solution.py
@@ -2,6 +2,15 @@
 import jax.numpy as jnp
 from jax import lax
 from jax.sharding import PartitionSpec as P
+
+
+def sum_by_hops(block, name):
+    peers = lax.axis_size(name)
+    summed, reach = (block, 1)
+    while reach < peers:
+        summed = summed + lax.ppermute(summed, name, [(i, i ^ reach) for i in range(peers)])
+        reach = 2 * reach
+    return summed
 
 
 def local(amplitudes, integrals, block_mask):
@@ -22,7 +31,7 @@
         precision=lax.Precision.HIGHEST,
         preferred_element_type=jnp.float32,
     )
-    summed = lax.psum(partial_terms, "ctr")
+    summed = sum_by_hops(partial_terms, "ctr")
     own_rows = summed.shape[0] // lax.axis_size("ctr")
     offset = lax.axis_index("ctr") * own_rows
     result = lax.dynamic_slice_in_dim(summed, offset, own_rows, 0)

time: 416 us -> 687 us (1.65)
  waiting for transfers between devices: 264 us -> 515 us
  other arithmetic: 0.69 us -> 10.3 us
  starting transfers between devices: 0.04 us -> 9.16 us
    ppermute x0 -> x5, waiting for transfers between devices: none -> 364 us  [sum_by_hops(): lax.ppermute(summed, name, [(i, i ^ reach) for i in range(peers)])]
    psum x1 -> x0, waiting for transfers between devices: 113 us -> none  [local(): summed = lax.psum(partial_terms, 'ctr')]
    add x0 -> x5, other arithmetic: none -> 10.3 us  [sum_by_hops(): summed + lax.ppermute(summed, name, [(i, i ^ reach) for i in range(peers)])]
    ppermute x0 -> x5, starting transfers between devices: none -> 9.16 us  [sum_by_hops(): lax.ppermute(summed, name, [(i, i ^ reach) for i in range(peers)])]
  transfers between devices with their start and end apart: 2 -> 6, of which waited for: 2 -> 6; matrix products, arithmetic and copies ran while one was open for 0% -> 0% of each run, Pallas kernels for 0% -> 0%
where the time goes in v2:
time: 687 us; the launch traced here: 684 us
  waiting for transfers between devices  515 us (75%)
  matrix products  72.9 us (11%)
  blocking collectives  60.3 us (9%)
  between operations  13.4 us (2%)
  other arithmetic  10.3 us (1%)
  starting transfers between devices  9.16 us (1%)
    ppermute x5, waiting for transfers between devices, sum_by_hops(): lax.ppermute(summed, name, [(i, i ^ reach) for i in range(peers)])  364 us
    all_gather x1, waiting for transfers between devices, local(): lax.all_gather(local_rows, 'outer', axis=0, tiled=True)  151 us
    dot_general x1, matrix products, local(): lax.dot_general(lax.all_gather(local_rows, 'outer', axis=0, tiled=True),...  72.9 us
    all_to_all x1, blocking collectives, local(): lax.all_to_all(amplitudes, 'ctr', split_axis=1, concat_axis=0, tiled=True)  60.3 us
  transfers between devices with their start and end apart: 6, of which 6 were waited for; matrix products, arithmetic and copies ran while one was open for 0% of the time, Pallas kernels for 0%

profile of v2, /device:TPU:1, one launch (start us, length us, event | category | flops | bytes accessed | tf_op | source)
XLA Modules:
  0.0 684.0 jit_solution(11176744206911725345)
XLA Ops:
  6.5 0.0 all-gather.2.cloned.1.call-start
  6.5 60.3 %all_to_all.19 = f32[8,32,4096]{2,0,1:T(8,128)} all-to-all(f32[8,32,4096]{2,0,1:T(8,128)} %bitcast.20), channel_id=1, replica_groups=mesh['outer'=4,'ctr'=32] {'ctr'}, dimensions={1} | all-to-all | bytes 8388608 | tf_op jit(solution)/shard_map/all_to_all | solution.py:26
  66.8 0.0 copy-start
  66.8 0.0 all-gather.2.cloned.1.call-update
  66.9 0.7 copy-done
  67.5 150.9 %all-gather.2.cloned.1.call-done = f32[1024,4096]{1,0:T(8,128)} async-done(((f32[256,4096]{1,0:T(8,128)}), f32[1024,4096]{1,0:T(8,128)}) %all-gather.2.cloned.1.call-update) | async-done | bytes 16777232 | tf_op jit(solution)/shard_map/all_gather | solution.py:28
  218.4 2.2 mul.14
  220.6 72.9 %fusion.2 = f32[1024,1024]{1,0:T(8,128)} fusion(f32[1024,4096]{1,0:T(8,128)} %all-gather.2.cloned.1.call-done, f32[1024,4096]{1,0:T(8,128)} %param.4, f32[128,8,32,128]{3,2,1,0:T(8,128)S(1)} %bitcast.18), kind=kOutput, calls=%fused_computation.3 | convolution fusion | flops 51543801856 | bytes 54525952 | tf_op jit(solution)/shard_map/dot_general | solution.py:27
  293.5 0.8 collective-permute-start
  294.3 7.0 %collective-permute-done = f32[1024,1024]{1,0:T(8,128)S(1)} collective-permute-done((f32[1024,1024]{1,0:T(8,128)}, f32[1024,1024]{1,0:T(8,128)S(1)}, u32[]{:S(2)}, u32[]{:S(2)}) %collective-permute-start) | collective-permute-done | bytes 4194336 | tf_op jit(solution)/shard_map/ppermute | solution.py:11
  301.3 3.1 add.18
  304.4 1.4 collective-permute-start.1
  305.8 90.5 %collective-permute-done.1 = f32[1024,1024]{1,0:T(8,128)S(1)} collective-permute-done((f32[1024,1024]{1,0:T(8,128)S(1)}, f32[1024,1024]{1,0:T(8,128)S(1)}, u32[]{:S(2)}, u32[]{:S(2)}) %collective-permute-start.1) | collective-permute-done | bytes 4194336 | tf_op jit(solution)/shard_map/ppermute | solution.py:11
  396.3 1.4 add.19
  397.6 3.0 collective-permute-start.2
  400.6 89.5 %collective-permute-done.2 = f32[1024,1024]{1,0:T(8,128)S(1)} collective-permute-done((f32[1024,1024]{1,0:T(8,128)S(1)}, f32[1024,1024]{1,0:T(8,128)S(1)}, u32[]{:S(2)}, u32[]{:S(2)}) %collective-permute-start.2) | collective-permute-done | bytes 4194336 | tf_op jit(solution)/shard_map/ppermute | solution.py:11
  490.1 1.4 add.20
  491.5 1.3 collective-permute-start.3
  492.8 88.8 %collective-permute-done.3 = f32[1024,1024]{1,0:T(8,128)S(1)} collective-permute-done((f32[1024,1024]{1,0:T(8,128)S(1)}, f32[1024,1024]{1,0:T(8,128)S(1)}, u32[]{:S(2)}, u32[]{:S(2)}) %collective-permute-start.3) | collective-permute-done | bytes 4194336 | tf_op jit(solution)/shard_map/ppermute | solution.py:11
  581.6 2.9 add.21
  584.5 2.7 collective-permute-start.4
  587.2 88.3 %collective-permute-done.4 = f32[1024,1024]{1,0:T(8,128)} collective-permute-done((f32[1024,1024]{1,0:T(8,128)}, f32[1024,1024]{1,0:T(8,128)}, u32[]{:S(2)}, u32[]{:S(2)}) %collective-permute-start.4) | collective-permute-done | bytes 4194336 | tf_op jit(solution)/shard_map/ppermute | solution.py:11
  675.5 1.6 dynamic-slice_add_fusion
  (1 shorter events, 0.0 us)
Async XLA Ops:
  6.5 211.9 %all-gather.2.cloned.1.call-start = ((), (), s32[]{:S(2)}) async-start(), calls=%async_computation.1 | async-start | bytes 20971520 | tf_op jit(solution)/shard_map/all_gather | solution.py:28
  66.8 0.7 copy-start
  293.5 7.8 %collective-permute-start = (f32[1024,1024]{1,0:T(8,128)}, f32[1024,1024]{1,0:T(8,128)S(1)}, u32[]{:S(2)}, u32[]{:S(2)}) collective-permute-start(f32[1024,1024]{1,0:T(8,128)} %fusion.2), channel_id=1, source_target_pairs={{0,1},{1,0},{2,3},{3,2},{4,5},{5,4},{6,7},{7,6},{8,9},{9,8},{10,11... | collective-permute-start | bytes 12582920 | tf_op jit(solution)/shard_map/ppermute | solution.py:11
  304.4 91.8 %collective-permute-start.1 = (f32[1024,1024]{1,0:T(8,128)S(1)}, f32[1024,1024]{1,0:T(8,128)S(1)}, u32[]{:S(2)}, u32[]{:S(2)}) collective-permute-start(f32[1024,1024]{1,0:T(8,128)S(1)} %add.18), channel_id=1, source_target_pairs={{0,2},{1,3},{2,0},{3,1},{4,6},{5,7},{6,4},{7,5},{8,10},{9,11},{10,... | collective-permute-start | bytes 12582920 | tf_op jit(solution)/shard_map/ppermute | solution.py:11
  397.6 92.5 %collective-permute-start.2 = (f32[1024,1024]{1,0:T(8,128)S(1)}, f32[1024,1024]{1,0:T(8,128)S(1)}, u32[]{:S(2)}, u32[]{:S(2)}) collective-permute-start(f32[1024,1024]{1,0:T(8,128)S(1)} %add.19), channel_id=1, source_target_pairs={{0,4},{1,5},{2,6},{3,7},{4,0},{5,1},{6,2},{7,3},{8,12},{9,13},{10,... | collective-permute-start | bytes 12582920 | tf_op jit(solution)/shard_map/ppermute | solution.py:11
  491.5 90.1 %collective-permute-start.3 = (f32[1024,1024]{1,0:T(8,128)S(1)}, f32[1024,1024]{1,0:T(8,128)S(1)}, u32[]{:S(2)}, u32[]{:S(2)}) collective-permute-start(f32[1024,1024]{1,0:T(8,128)S(1)} %add.20), channel_id=1, source_target_pairs={{0,8},{1,9},{2,10},{3,11},{4,12},{5,13},{6,14},{7,15},{8,0},{9,1},... | collective-permute-start | bytes 12582920 | tf_op jit(solution)/shard_map/ppermute | solution.py:11
  584.5 91.0 %collective-permute-start.4 = (f32[1024,1024]{1,0:T(8,128)}, f32[1024,1024]{1,0:T(8,128)}, u32[]{:S(2)}, u32[]{:S(2)}) collective-permute-start(f32[1024,1024]{1,0:T(8,128)} %add.21), channel_id=1, source_target_pairs={{0,16},{1,17},{2,18},{3,19},{4,20},{5,21},{6,22},{7,23},{8,24},{9,... | collective-permute-start | bytes 12582920 | tf_op jit(solution)/shard_map/ppermute | solution.py:11
Sparse Core Ops, SparseCore 0:
  67.0 151.3 all-gather.1
